TPU v7x, 512 devices: a whole 4x4x16 slice. The times are simulated.
512 devices in a mesh: dp: 32 (over x_lo, z), mp: 16 (over y, x_hi, core).
Axes of the slice: x: 4 (x_hi: 2, x_lo: 2; x = x_hi * 2 + x_lo), y: 4, z: 16, core: 2. Of those that a mesh axis runs over, the one named last changes fastest.
Arguments:
- activations: bfloat16 [32, 1024, 512], P('dp', 'mp'), may hold values from -6 to 6
- filters: bfloat16 [27, 1024, 1024], P(None, 'mp', 'dp'), may hold values from -0.0390625 to 0.0390625
- bias: float32 [1024], P('mp'), may hold values from -3 to 3
Outputs:
- features: bfloat16 [32, 1024, 512], P('dp', 'mp')
All inputs are finite; a program needn't handle non-finite values.
Results may differ from a plain program's by a relative error of at most 0.001.
Values may be sent and summed in bfloat16 or wider, within the bound.
No kernel may reach another device: no remote copies, remote signals or barrier semaphores. Data moves between devices by JAX's collectives and lax.ppermute only.
A program may use at most 128 MiB of HBM per device.

v0:
```python
import jax
import jax.numpy as jnp
from jax import lax
from jax.sharding import PartitionSpec as P

SX = 2
SY = 16
SZ = 16


def stacked_taps(values):
    cells = SX * SY * SZ
    margin = SY * SZ + SZ + 1
    extended = jnp.pad(values, ((0, 0), (margin, margin)))
    place = jnp.arange(cells, dtype=jnp.int32)
    first_pos = place // (SY * SZ)
    second_pos = place // SZ % SY
    third_pos = place % SZ
    copies = []
    for off_a in (-1, 0, 1):
        for off_b in (-1, 0, 1):
            for off_c in (-1, 0, 1):
                offset = off_a * SY * SZ + off_b * SZ + off_c
                moved = extended[:, margin + offset : margin + offset + cells]
                first = first_pos + off_a
                second = second_pos + off_b
                third = third_pos + off_c
                inside = (
                    (first >= 0)
                    & (first < SX)
                    & (second >= 0)
                    & (second < SY)
                    & (third >= 0)
                    & (third < SZ)
                )
                copies.append(jnp.where(inside[None, :], moved, jnp.zeros_like(moved)))
    return jnp.concatenate(copies, axis=0)


def add_taps(weights, inputs):
    taps_count, out_rows, chans = weights.shape
    flat_weights = jnp.transpose(weights, (1, 0, 2)).reshape(out_rows, taps_count * chans)
    return jnp.dot(flat_weights, stacked_taps(inputs), preferred_element_type=jnp.float32)


def per_device(activations, filters, bias):
    all_filters = lax.all_gather(filters, "dp", axis=2, tiled=True)
    summed = add_taps(all_filters, lax.all_gather(activations, "mp", axis=1, tiled=True)[0])
    value = summed + bias[:, None]
    result = jnp.where(value > 0, value, 0.3 * value).astype(jnp.bfloat16)
    return result[None]


def solution(mesh):
    in_specs = (P("dp", "mp", None), P(None, "mp", "dp"), P("mp"))
    out_specs = P("dp", "mp", None)
    return jax.shard_map(
        per_device, mesh=mesh, in_specs=in_specs, out_specs=out_specs, check_vma=False
    )
```

profile of v0, /device:TPU:8, one launch (start us, length us, event | category | flops | bytes accessed | tf_op | source)
XLA Modules:
  0.0 245.5 jit_solution(933689072745846719)
XLA Ops:
  6.5 0.0 all-gather.3.cloned.1.call-start
  6.5 0.7 all-gather.3.cloned.1.call-update
  7.3 0.0 all-gather.5.cloned.1.call-start
  7.3 0.7 all-gather.5.cloned.1.call-update
  8.4 66.4 %all-gather.3.cloned.1.call-done = bf16[1,1024,512]{2,1,0:T(8,128)(2,1)} async-done(((bf16[1,64,512]{2,1,0:T(8,128)(2,1)}), bf16[1,1024,512]{2,1,0:T(8,128)(2,1)}) %all-gather.3.cloned.1.call-update) | async-done | bytes 1048592 | tf_op jit(solution)/shard_map/all_gather | solution.py:48
  74.8 0.0 copy-start
  74.8 0.0 copy-start.1
  74.8 2.3 fusion.2
  77.2 2.4 fusion.4
  79.6 2.4 fusion.6
  82.0 2.4 fusion.8
  84.4 2.3 fusion.10
  86.7 2.6 %fusion.12 = bf16[27648,512]{1,0:T(8,128)(2,1)} fusion(bf16[27648,512]{1,0:T(8,128)(2,1)} %fusion.10, bf16[1024,512]{1,0:T(8,128)(2,1)} %bitcast.22, pred[512]{0:T(512)(128)(4,1)S(1)} %and_and_fusion.28), kind=kLoop, calls=%fused_computation.39 | loop fusion | flops 524288 | bytes 2097664
  89.3 2.6 %fusion.14 = bf16[27648,512]{1,0:T(8,128)(2,1)} fusion(bf16[27648,512]{1,0:T(8,128)(2,1)} %fusion.12, bf16[1024,512]{1,0:T(8,128)(2,1)} %bitcast.23, pred[512]{0:T(512)(128)(4,1)S(1)} %and_and_fusion.26), kind=kLoop, calls=%fused_computation.41 | loop fusion | flops 524288 | bytes 2097664
  91.9 2.7 %fusion.16 = bf16[27648,512]{1,0:T(8,128)(2,1)} fusion(bf16[27648,512]{1,0:T(8,128)(2,1)} %fusion.14, bf16[1024,512]{1,0:T(8,128)(2,1)} %bitcast.24, pred[512]{0:T(512)(128)(4,1)S(1)} %and_and_fusion.25), kind=kLoop, calls=%fused_computation.43 | loop fusion | flops 524288 | bytes 2097664
  94.5 2.6 %fusion.18 = bf16[27648,512]{1,0:T(8,128)(2,1)} fusion(bf16[27648,512]{1,0:T(8,128)(2,1)} %fusion.16, bf16[1024,512]{1,0:T(8,128)(2,1)} %bitcast.25, pred[512]{0:T(512)(128)(4,1)S(1)} %and_and_fusion.24), kind=kLoop, calls=%fused_computation.45 | loop fusion | flops 524288 | bytes 2097664
  97.2 2.7 %fusion.20 = bf16[27648,512]{1,0:T(8,128)(2,1)} fusion(bf16[27648,512]{1,0:T(8,128)(2,1)} %fusion.18, bf16[1024,512]{1,0:T(8,128)(2,1)} %bitcast.26, pred[512]{0:T(512)(128)(4,1)S(1)} %and_and_fusion.22), kind=kLoop, calls=%fused_computation.47 | loop fusion | flops 524288 | bytes 2097664
  99.9 2.8 %fusion.22 = bf16[27648,512]{1,0:T(8,128)(2,1)} fusion(bf16[27648,512]{1,0:T(8,128)(2,1)} %fusion.20, bf16[1024,512]{1,0:T(8,128)(2,1)} %bitcast.27, pred[512]{0:T(512)(128)(4,1)S(1)} %and_and_fusion.21), kind=kLoop, calls=%fused_computation.49 | loop fusion | flops 524288 | bytes 2097664
  102.6 2.8 %fusion.24 = bf16[27648,512]{1,0:T(8,128)(2,1)} fusion(bf16[27648,512]{1,0:T(8,128)(2,1)} %fusion.22, bf16[1024,512]{1,0:T(8,128)(2,1)} %bitcast.28, pred[512]{0:T(512)(128)(4,1)S(1)} %and_and_fusion.20), kind=kLoop, calls=%fused_computation.51 | loop fusion | flops 524288 | bytes 2097664
  105.4 2.8 %fusion.26 = bf16[27648,512]{1,0:T(8,128)(2,1)} fusion(bf16[27648,512]{1,0:T(8,128)(2,1)} %fusion.24, bf16[1024,512]{1,0:T(8,128)(2,1)} %bitcast.29, pred[512]{0:T(512)(128)(4,1)S(1)} %and_and_fusion.18), kind=kLoop, calls=%fused_computation.53 | loop fusion | flops 524288 | bytes 2097664
  108.2 2.4 select_dynamic-update-slice_fusion
  110.6 0.0 copy-done
  110.6 1.5 fusion.28
  112.1 1.5 fusion.30
  113.6 1.5 fusion.32
  115.1 1.5 fusion.34
  116.6 1.3 fusion.36
  118.0 1.3 fusion.38
  119.3 1.3 fusion.40
  120.6 1.4 fusion.42
  122.0 1.1 fusion.44
  123.1 1.3 fusion.46
  124.4 1.3 fusion.48
  125.7 1.2 fusion.50
  126.9 1.2 fusion.52
  128.1 94.0 %all-gather.5.cloned.1.call-done = bf16[27,64,1024]{1,2,0:T(8,128)(2,1)} async-done(((bf16[27,64,32]{1,2,0:T(8,128)(2,1)}), bf16[27,64,1024]{1,2,0:T(8,128)(2,1)}) %all-gather.5.cloned.1.call-update) | async-done | bytes 3538960 | tf_op jit(solution)/shard_map/all_gather | solution.py:47
  222.2 0.0 copy-done.1
  222.2 16.5 %fusion.54 = bf16[1,64,512]{2,1,0:T(8,128)(2,1)} fusion(bf16[27648,512]{1,0:T(8,128)(2,1)} %fusion.52, bf16[64,27648]{0,1:T(8,128)(2,1)} %bitcast.43, f32[64]{0:T(128)S(1)} %copy-done.1), kind=kOutput, calls=%fused_computation.83 | convolution fusion | flops 1812103168 | bytes 31916288 | tf_op jit(solution)/shard_map/dot_general | solution.py:43
  (27 shorter events, 0.3 us)
Async XLA Ops:
  6.5 68.3 %all-gather.3.cloned.1.call-start = ((), (), s32[]{:S(2)}) async-start(), calls=%async_computation | async-start | bytes 1114112 | tf_op jit(solution)/shard_map/all_gather | solution.py:48
  7.3 214.9 %all-gather.5.cloned.1.call-start = ((), (), s32[]{:S(2)}) async-start(), calls=%async_computation.1 | async-start | bytes 7299072 | tf_op jit(solution)/shard_map/all_gather | solution.py:47
  74.8 35.8 %copy-start = (bf16[1,1024,512]{2,1,0:T(8,128)(2,1)S(1)}, bf16[1,1024,512]{2,1,0:T(8,128)(2,1)}, u32[]{:S(2)}) copy-start(bf16[1,1024,512]{2,1,0:T(8,128)(2,1)} %all-gather.3.cloned.1.call-done) | copy-start | bytes 3145732
  74.8 147.3 %copy-start.1 = (f32[64]{0:T(128)S(1)}, f32[64]{0:T(128)}, u32[]{:S(2)}) copy-start(f32[64]{0:T(128)} %param.5) | copy-start | bytes 772
Sparse Core Ops, SparseCore 0:
  10.7 64.1 all-gather.2
  76.9 145.1 all-gather.4
where the time goes:
time: 246 us
  waiting for transfers between devices  162 us (66%)
  other arithmetic  53.6 us (22%)
  matrix products  16.5 us (7%)
  between operations  13.5 us (5%)
    all_gather x1, waiting for transfers between devices, per_device(): all_filters = lax.all_gather(filters, 'dp', axis=2, tiled=True)  94 us
    all_gather x1, waiting for transfers between devices, per_device(): lax.all_gather(activations, 'mp', axis=1, tiled=True)[0]  66.4 us
    unnamed x26, other arithmetic  52 us
    dot_general x1, matrix products, add_taps(): jnp.dot(flat_weights, stacked_taps(inputs), preferred_element_type=jnp.fl...  16.5 us
  transfers between devices with their start and end apart: 2, of which 2 were waited for; matrix products, arithmetic and copies ran while one was open for 22% of the time, Pallas kernels for 0%

commit v1 on v0

--- a/solution.py
+++ b/solution.py
@@ -6,6 +6,11 @@
 SX = 2
 SY = 16
 SZ = 16
+
+
+def swapped_in(x, name, along):
+    outgoing = jnp.stack([x] * lax.axis_size(name))
+    return jnp.concatenate(lax.all_to_all(outgoing, name, 0, 0), axis=along)
 
 
 def stacked_taps(values):
@@ -45,7 +50,7 @@
 
 def per_device(activations, filters, bias):
     all_filters = lax.all_gather(filters, "dp", axis=2, tiled=True)
-    summed = add_taps(all_filters, lax.all_gather(activations, "mp", axis=1, tiled=True)[0])
+    summed = add_taps(all_filters, swapped_in(activations, "mp", 1)[0])
     value = summed + bias[:, None]
     result = jnp.where(value > 0, value, 0.3 * value).astype(jnp.bfloat16)
     return result[None]

time: 246 us -> 193 us (0.78)
  waiting for transfers between devices: 162 us -> 114 us
  other arithmetic: 53.6 us -> 36.7 us
  starting transfers between devices: 0.04 us -> 9.29 us
    all_gather x1 -> x0, waiting for transfers between devices: 66.4 us -> none  [per_device(): lax.all_gather(activations, 'mp', axis=1, tiled=True)[0]]
    unnamed x26, other arithmetic: 52 us -> 35.2 us
    all_to_all x0 -> x1, waiting for transfers between devices: none -> 14.2 us  [swapped_in(): return jnp.concatenate(lax.all_to_all(outgoing, name, 0, 0), axis=along)]
    all_to_all x0 -> x1, starting transfers between devices: none -> 9.26 us  [swapped_in(): return jnp.concatenate(lax.all_to_all(outgoing, name, 0, 0), axis=along)]
    all_gather x1, waiting for transfers between devices: 94 us -> 99.4 us  [per_device(): all_filters = lax.all_gather(filters, 'dp', axis=2, tiled=True)]
  transfers between devices with their start and end apart: 2 -> 2, of which waited for: 2 -> 2; matrix products, arithmetic and copies ran while one was open for 22% -> 19% of each run, Pallas kernels for 0% -> 0%
where the time goes in v1:
time: 193 us; the launch traced here: 192 us
  waiting for transfers between devices  114 us (59%)
  other arithmetic  36.7 us (19%)
  matrix products  16.5 us (9%)
  between operations  13.5 us (7%)
  starting transfers between devices  9.29 us (5%)
    all_gather x1, waiting for transfers between devices, per_device(): all_filters = lax.all_gather(filters, 'dp', axis=2, tiled=True)  99.4 us
    unnamed x26, other arithmetic  35.2 us
    dot_general x1, matrix products, add_taps(): jnp.dot(flat_weights, stacked_taps(inputs), preferred_element_type=jnp.fl...  16.5 us
    all_to_all x1, waiting for transfers between devices, swapped_in(): return jnp.concatenate(lax.all_to_all(outgoing, name, 0, 0), axis=along)  14.2 us
    all_to_all x1, starting transfers between devices, swapped_in(): return jnp.concatenate(lax.all_to_all(outgoing, name, 0, 0), axis=along)  9.26 us
  transfers between devices with their start and end apart: 2, of which 2 were waited for; matrix products, arithmetic and copies ran while one was open for 19% of the time, Pallas kernels for 0%

profile of v1, /device:TPU:8, one launch (start us, length us, event | category | flops | bytes accessed | tf_op | source)
XLA Modules:
  0.0 192.3 jit_solution(8989374907668469236)
XLA Ops:
  6.5 1.9 stack.2
  8.4 9.3 %all-to-all-start = ((bf16[16,1,64,512]{3,2,1,0:T(8,128)(2,1)}), bf16[16,1,64,512]{3,2,1,0:T(8,128)(2,1)S(1)}, u32[]{:S(2)}, u32[]{:S(2)}) async-start(bf16[16,1,64,512]{3,2,1,0:T(8,128)(2,1)} %stack.2), calls=%async_computation | async-start | bytes 2097152 | tf_op jit(solution)/shard_map/all_to_all | solution.py:13
  17.7 0.0 all-gather.2.cloned.1.call-start
  17.8 0.7 all-gather.2.cloned.1.call-update
  18.9 14.2 %all-to-all-done = bf16[16,1,64,512]{3,2,1,0:T(8,128)(2,1)S(1)} async-done(((bf16[16,1,64,512]{3,2,1,0:T(8,128)(2,1)}), bf16[16,1,64,512]{3,2,1,0:T(8,128)(2,1)S(1)}, u32[]{:S(2)}, u32[]{:S(2)}) %all-to-all-start) | async-done | bytes 1048608 | tf_op jit(solution)/shard_map/all_to_all | solution.py:13
  33.1 0.0 copy-start
  33.1 1.2 fusion.2
  34.3 1.3 fusion.4
  35.6 1.2 fusion.6
  36.8 1.2 fusion.8
  38.0 1.1 fusion.10
  39.1 1.4 fusion.12
  40.5 1.4 fusion.14
  41.9 1.4 fusion.16
  43.3 1.4 fusion.18
  44.7 1.5 fusion.20
  46.2 1.5 fusion.22
  47.8 1.5 fusion.24
  49.3 1.6 fusion.26
  50.9 1.2 select_dynamic-update-slice_fusion
  52.0 1.5 fusion.28
  53.6 1.5 fusion.30
  55.0 1.5 fusion.32
  56.5 1.5 fusion.34
  58.1 1.3 fusion.36
  59.4 1.3 fusion.38
  60.7 1.3 fusion.40
  62.0 1.3 fusion.42
  63.4 1.1 fusion.44
  64.5 1.3 fusion.46
  65.7 1.3 fusion.48
  67.0 1.2 fusion.50
  68.3 1.2 fusion.52
  69.5 99.4 %all-gather.2.cloned.1.call-done = bf16[27,64,1024]{1,2,0:T(8,128)(2,1)} async-done(((bf16[27,64,32]{1,2,0:T(8,128)(2,1)}), bf16[27,64,1024]{1,2,0:T(8,128)(2,1)}) %all-gather.2.cloned.1.call-update) | async-done | bytes 3538960 | tf_op jit(solution)/shard_map/all_gather | solution.py:52
  168.9 0.0 copy-done
  168.9 16.5 %fusion.54 = bf16[1,64,512]{2,1,0:T(8,128)(2,1)} fusion(bf16[27648,512]{1,0:T(8,128)(2,1)} %fusion.52, bf16[64,27648]{0,1:T(8,128)(2,1)} %bitcast.44, f32[64]{0:T(128)S(1)} %copy-done), kind=kOutput, calls=%fused_computation.83 | convolution fusion | flops 1812103168 | bytes 31916288 | tf_op jit(solution)/shard_map/dot_general | solution.py:48
  (27 shorter events, 0.3 us)
Async XLA Ops:
  8.4 24.6 %all-to-all-start = ((bf16[16,1,64,512]{3,2,1,0:T(8,128)(2,1)}), bf16[16,1,64,512]{3,2,1,0:T(8,128)(2,1)S(1)}, u32[]{:S(2)}, u32[]{:S(2)}) async-start(bf16[16,1,64,512]{3,2,1,0:T(8,128)(2,1)} %stack.2), calls=%async_computation | async-start | bytes 2097152 | tf_op jit(solution)/shard_map/all_to_all | solution.py:13
  17.7 151.2 %all-gather.2.cloned.1.call-start = ((), (), s32[]{:S(2)}) async-start(), calls=%async_computation.1 | async-start | bytes 7299072 | tf_op jit(solution)/shard_map/all_gather | solution.py:52
  33.1 135.9 %copy-start = (f32[64]{0:T(128)S(1)}, f32[64]{0:T(128)}, u32[]{:S(2)}) copy-start(f32[64]{0:T(128)} %param.5) | copy-start | bytes 772
Sparse Core Ops, SparseCore 0:
  20.6 148.2 all-gather.1
